TPU v7x, 256 devices: a whole 4x4x8 slice. The times are simulated.
256 devices in a mesh: row: 8 (over x, core), col: 32 (over z, y).
Axes of the slice: x: 4, y: 4, z: 8, core: 2. Of those that a mesh axis runs over, the one named last changes fastest.
Arguments:
- features: float32 [32768, 512], P(('col', 'row')), may hold values from -6 to 6
- weight: float32 [512, 512], replicated, may hold values from -0.25 to 0.25
- cotangent: bfloat16 [32768, 512], P(('row', 'col')), may hold values from -6 to 6
- block_values: bfloat16 [8, 32, 96, 128, 128], P('row', 'col'), may hold values from -0.0625 to 0.0625
- block_coords: int32 [8, 32, 2, 96], P('row', 'col'), may hold values from -1 to 31, as said below
Outputs:
- activated: float32 [32768, 512], P(('row', 'col'))
- dfeatures: float32 [32768, 512], P(('col', 'row'))
- dweight: float32 [512, 512], P('row', 'col')
Inputs may be any that keep to these rules, and one draw needn't show every extreme that they name: block_coords[r, c, 0, s] is a block row below 32 and block_coords[r, c, 1, s] a block column below 8 of slot s of device (r, c), or both are -1 for an unused slot. Used slots come first and name distinct blocks; each device uses between a quarter of 96 (rounded down) and all 96 slots, and some device uses all 96.
All inputs are finite; a program needn't handle non-finite values.
Results may differ from a plain program's by a relative error of at most 0.006.
Values may be sent and summed in bfloat16 or wider, within the bound.
No kernel may reach another device: no remote copies, remote signals or barrier semaphores. Data moves between devices by JAX's collectives and lax.ppermute only.
A program may use at most 128 MiB of HBM per device.

v0:
```python
import jax
import jax.numpy as jnp
from jax import lax
from jax.sharding import PartitionSpec as P


def silu_slope(values):
    sigma = jax.nn.sigmoid(values)
    return sigma * (1.0 + values * (1.0 - sigma))


def group_size():
    return 32


def blocks_forward(slot_values, slot_rows, slot_cols, tile_stack, out_blocks):
    slot_count = slot_values.shape[0]
    group = group_size()
    turn_count = slot_count // group
    block = slot_values.shape[1]
    hidden_width = tile_stack.shape[-1]

    def add_group(totals, slot_item):
        group_vals, row_ids, col_ids = slot_item
        selected = jnp.take(tile_stack, col_ids, axis=0)
        products = jnp.einsum(
            "sab,sbc->sac", group_vals, selected, preferred_element_type=jnp.float32
        )
        return (totals.at[row_ids].add(products), None)

    zero_sums = jnp.zeros((out_blocks, block, hidden_width), jnp.float32)
    totals, _ = lax.scan(
        add_group,
        zero_sums,
        (
            slot_values.reshape(turn_count, group, block, block),
            slot_rows.reshape(turn_count, group),
            slot_cols.reshape(turn_count, group),
        ),
    )
    return totals.reshape(out_blocks * block, hidden_width)


def blocks_backward(slot_values, slot_rows, slot_cols, tile_stack, out_blocks):
    slot_count = slot_values.shape[0]
    group = group_size()
    turn_count = slot_count // group
    block = slot_values.shape[1]
    hidden_width = tile_stack.shape[-1]

    def add_group(totals, slot_item):
        group_vals, row_ids, col_ids = slot_item
        selected = jnp.take(tile_stack, row_ids, axis=0)
        products = jnp.einsum(
            "sab,sac->sbc", group_vals, selected, preferred_element_type=jnp.float32
        )
        return (totals.at[col_ids].add(products), None)

    zero_sums = jnp.zeros((out_blocks, block, hidden_width), jnp.float32)
    totals, _ = lax.scan(
        add_group,
        zero_sums,
        (
            slot_values.reshape(turn_count, group, block, block),
            slot_rows.reshape(turn_count, group),
            slot_cols.reshape(turn_count, group),
        ),
    )
    return totals.reshape(out_blocks * block, hidden_width)


def on_device(features, weight, cotangent, block_values, block_coords):
    slot_values = block_values[0, 0]
    coordinate = block_coords[0, 0]
    live_slots = coordinate[0] >= 0
    slot_values = jnp.where(live_slots[:, None, None], slot_values, jnp.zeros_like(slot_values))
    slot_rows = jnp.maximum(coordinate[0], 0)
    slot_cols = jnp.maximum(coordinate[1], 0)
    block = slot_values.shape[1]
    own_rows = features.shape[0]
    hidden_width = features.shape[1]
    col_count = lax.axis_size("col")
    row_count = lax.axis_size("row")
    row_blocks = col_count * own_rows // block
    col_blocks = row_count * own_rows // block
    gathered_cot = lax.all_gather(cotangent, "col", axis=0, tiled=True)
    xcopy = features.astype(jnp.bfloat16)
    wcopy = weight.astype(jnp.bfloat16)
    projected = jnp.dot(xcopy, wcopy, preferred_element_type=jnp.float32).astype(jnp.bfloat16)
    column_rows = lax.all_gather(projected, "row", axis=0, tiled=True)
    partial_value = blocks_forward(
        slot_values,
        slot_rows,
        slot_cols,
        column_rows.reshape(col_blocks, block, hidden_width),
        row_blocks,
    )
    full_sums = lax.psum(partial_value, "col")
    row_start = lax.axis_index("col") * own_rows
    own_sums = lax.dynamic_slice_in_dim(full_sums, row_start, own_rows, 0)
    activated = jax.nn.silu(own_sums)
    slope_rows = (gathered_cot.astype(jnp.float32) * silu_slope(full_sums)).astype(jnp.bfloat16)
    column_part = blocks_backward(
        slot_values,
        slot_rows,
        slot_cols,
        slope_rows.reshape(row_blocks, block, hidden_width),
        col_blocks,
    )
    node_grad = lax.psum_scatter(column_part, "row", scatter_dimension=0, tiled=True)
    grad_copy = node_grad.astype(jnp.bfloat16)
    dfeatures = jnp.dot(grad_copy, wcopy.T, preferred_element_type=jnp.float32)
    local_weight = jnp.dot(xcopy.T, grad_copy, preferred_element_type=jnp.float32)
    weight_part = lax.psum_scatter(local_weight, "row", scatter_dimension=0, tiled=True)
    node_total = own_rows * row_count * col_count
    dweight = lax.psum_scatter(weight_part, "col", scatter_dimension=1, tiled=True) * (
        1.0 / node_total**0.5
    )
    return (activated, dfeatures, dweight)


def solution(mesh):
    placed = (
        P(("col", "row"), None),
        P(),
        P(("row", "col"), None),
        P("row", "col", None, None, None),
        P("row", "col", None, None),
    )
    return jax.shard_map(
        on_device,
        mesh=mesh,
        in_specs=placed,
        out_specs=(P(("row", "col"), None), P(("col", "row"), None), P("row", "col")),
        check_vma=False,
    )
```

profile of v0, /device:TPU:2, one launch (start us, length us, event | category | flops | bytes accessed | tf_op | source)
XLA Modules:
  0.0 720.8 jit_solution(8900149121695483579)
XLA Ops:
  16.8 20.7 %all-gather.3.cloned.1.call-done = bf16[1024,512]{1,0:T(8,128)(2,1)} async-done(((bf16[128,512]{1,0:T(8,128)(2,1)}), bf16[1024,512]{1,0:T(8,128)(2,1)}) %all-gather.3.cloned.1.call-update) | async-done | bytes 1048592 | tf_op jit(solution)/shard_map/all_gather | solution.py:90
  37.6 4.3 broadcast_in_dim.40
  41.9 86.4 %while.20 = (s32[]{:T(128)}, f32[32,128,512]{2,1,0:T(8,128)}, s32[3,32]{1,0:T(4,128)S(1)}, bf16[3,32,128,128]{2,3,1,0:T(8,128)(2,1)}, s32[3,32]{1,0:T(4,128)S(1)}, /*index=5*/bf16[8,128,512]{2,1,0:T(8,128)(2,1)S(1)}, s32[]{:T(128)}) while((s32[]{:T(128)}, f32[32,128,512]{2,1,0:T(8,128)}, s32[3,32]{1,0:T(4,128)S(1)}, ...), condition=%wide.region_2.3_spmd, body=%wide.region_0.2_spmd.sunk | while | flops 541066624 | bytes 47191200 | solution.py:32
  44.7 7.1 fusion.40
  51.8 18.9 %scatter_fusion = f32[32,128,512]{2,1,0:T(8,128)} fusion(f32[32,128,512]{2,1,0:T(8,128)} %get-tuple-element.201, s32[32]{0:T(128)S(1)} %get-tuple-element.183, f32[32,128,512]{2,1,0:T(8,128)} %fusion.40), kind=kCustom, calls=%fused_computation.2.clone.1 | custom fusion | flops 2097152 | bytes 25165952 | tf_op jit(solution)/shard_map/while/body/eval_jaxpr/scatter-add | solution.py:29
  73.5 7.1 fusion.40
  80.6 19.0 %scatter_fusion = f32[32,128,512]{2,1,0:T(8,128)} fusion(f32[32,128,512]{2,1,0:T(8,128)} %get-tuple-element.201, s32[32]{0:T(128)S(1)} %get-tuple-element.183, f32[32,128,512]{2,1,0:T(8,128)} %fusion.40), kind=kCustom, calls=%fused_computation.2.clone.1 | custom fusion | flops 2097152 | bytes 25165952 | tf_op jit(solution)/shard_map/while/body/eval_jaxpr/scatter-add | solution.py:29
  102.4 7.1 fusion.40
  109.5 18.8 %scatter_fusion = f32[32,128,512]{2,1,0:T(8,128)} fusion(f32[32,128,512]{2,1,0:T(8,128)} %get-tuple-element.201, s32[32]{0:T(128)S(1)} %get-tuple-element.183, f32[32,128,512]{2,1,0:T(8,128)} %fusion.40), kind=kCustom, calls=%fused_computation.2.clone.1 | custom fusion | flops 2097152 | bytes 25165952 | tf_op jit(solution)/shard_map/while/body/eval_jaxpr/scatter-add | solution.py:29
  128.4 213.3 %all-reduce.2.cloned.1.call-done = f32[4096,512]{1,0:T(8,128)} async-done(((f32[4096,512]{1,0:T(8,128)}), f32[4096,512]{1,0:T(8,128)}) %all-reduce.2.cloned.1.call-update) | async-done | bytes 8388624 | tf_op jit(solution)/shard_map/psum | solution.py:98
  341.7 7.6 %multiply_convert_fusion = bf16[4096,512]{1,0:T(8,128)(2,1)} fusion(f32[4096,512]{1,0:T(8,128)} %all-reduce.2.cloned.1.call-done, bf16[4096,512]{1,0:T(8,128)(2,1)} %all-gather.5.cloned.1.call-done), kind=kLoop, calls=%fused_computation.40 | loop fusion | flops 20971520 | bytes 16777216 | tf_op jit(solution)/shard_map/convert_element_type | solution.py:102
  349.6 71.1 %while.21 = (s32[]{:T(128)}, f32[8,128,512]{2,1,0:T(8,128)S(1)}, s32[3,32]{1,0:T(4,128)S(1)}, bf16[3,32,128,128]{2,3,1,0:T(8,128)(2,1)}, s32[3,32]{1,0:T(4,128)S(1)}, /*index=5*/bf16[32,128,512]{2,1,0:T(8,128)(2,1)}, s32[]{:T(128)}) while((s32[]{:T(128)}, f32[8,128,512]{2,1,0:T(8,128)S(1)}, s32[3,32]{1,0:T(4,128)S(1)}, ...), condition=%wide.region_6.7_spmd, body=%wide.region_4.6_spmd.sunk | while | flops 541066624 | bytes 47191200 | solution.py:60
  349.6 5.0 gather_fusion.1
  354.6 7.1 fusion.44
  361.7 11.8 %scatter_fusion.1 = f32[8,128,512]{2,1,0:T(8,128)S(1)} fusion(f32[8,128,512]{2,1,0:T(8,128)S(1)} %get-tuple-element.222, s32[32]{0:T(128)S(1)} %get-tuple-element.191, f32[32,128,512]{2,1,0:T(8,128)} %fusion.44), kind=kCustom, calls=%fused_computation.3.clone.1 | custom fusion | flops 2097152 | bytes 25165952 | tf_op jit(solution)/shard_map/while/body/eval_jaxpr/scatter-add | solution.py:57
  373.5 4.9 gather_fusion.1
  378.4 7.1 fusion.44
  385.5 11.6 %scatter_fusion.1 = f32[8,128,512]{2,1,0:T(8,128)S(1)} fusion(f32[8,128,512]{2,1,0:T(8,128)S(1)} %get-tuple-element.222, s32[32]{0:T(128)S(1)} %get-tuple-element.191, f32[32,128,512]{2,1,0:T(8,128)} %fusion.44), kind=kCustom, calls=%fused_computation.3.clone.1 | custom fusion | flops 2097152 | bytes 25165952 | tf_op jit(solution)/shard_map/while/body/eval_jaxpr/scatter-add | solution.py:57
  397.2 4.9 gather_fusion.1
  402.1 7.1 fusion.44
  409.2 11.5 %scatter_fusion.1 = f32[8,128,512]{2,1,0:T(8,128)S(1)} fusion(f32[8,128,512]{2,1,0:T(8,128)S(1)} %get-tuple-element.222, s32[32]{0:T(128)S(1)} %get-tuple-element.191, f32[32,128,512]{2,1,0:T(8,128)} %fusion.44), kind=kCustom, calls=%fused_computation.3.clone.1 | custom fusion | flops 2097152 | bytes 25165952 | tf_op jit(solution)/shard_map/while/body/eval_jaxpr/scatter-add | solution.py:57
  422.1 32.0 %reduce-scatter.6.cloned.1.call-done = f32[128,512]{1,0:T(8,128)} async-done(((f32[1024,512]{1,0:T(8,128)}), f32[128,512]{1,0:T(8,128)}) %reduce-scatter.6.cloned.1.call-update) | async-done | bytes 262160 | tf_op jit(solution)/shard_map/reduce_scatter | solution.py:110
  458.7 32.1 %reduce-scatter.10.cloned.1.call-done = f32[64,512]{1,0:T(8,128)} async-done(((f32[512,512]{1,0:T(8,128)}), f32[64,512]{1,0:T(8,128)}) %reduce-scatter.10.cloned.1.call-update) | async-done | bytes 131088
  493.6 219.0 %reduce-scatter.8.cloned.1.call-done = f32[64,16]{0,1:T(8,128)} async-done(((f32[64,512]{0,1:T(8,128)}), f32[64,16]{0,1:T(8,128)}) %reduce-scatter.8.cloned.1.call-update) | async-done | bytes 4112 | tf_op jit(solution)/shard_map/reduce_scatter | solution.py:116
  (61 shorter events, 28.5 us)
Async XLA Ops:
  7.2 7.4 %copy-start.5 = (s32[1,1,2,96]{3,2,1,0:T(2,128)S(1)}, s32[1,1,2,96]{3,2,1,0:T(2,128)}, u32[]{:S(2)}) copy-start(s32[1,1,2,96]{3,2,1,0:T(2,128)} %param.13) | copy-start | bytes 2308
  7.2 30.4 %all-gather.3.cloned.1.call-start = ((), (), s32[]{:S(2)}) async-start(), calls=%async_computation.3 | async-start | bytes 1179648 | tf_op jit(solution)/shard_map/all_gather | solution.py:90
  9.5 118.9 %all-gather.5.cloned.1.call-start = ((), (), s32[]{:S(2)}) async-start(), calls=%async_computation.5 | async-start | bytes 4325376 | tf_op jit(solution)/shard_map/all_gather | solution.py:86
  10.2 331.5 %all-reduce.2.cloned.1.call-start = ((), (), s32[]{:S(2)}) async-start(), calls=%async_computation.4 | async-start | bytes 16777216 | tf_op jit(solution)/shard_map/psum | solution.py:98
  37.6 4.3 copy-start.1
  128.3 325.9 %reduce-scatter.6.cloned.1.call-start = ((), (), s32[]{:S(2)}) async-start(), calls=%async_computation.6 | async-start | bytes 2359296 | tf_op jit(solution)/shard_map/reduce_scatter | solution.py:110
  349.6 104.6 %copy-start.3 = (f32[128,512]{1,0:T(8,128)S(1)}, f32[128,512]{1,0:T(8,128)}, u32[]{:S(2)}) copy-start(f32[128,512]{1,0:T(8,128)} %param.9) | copy-start | bytes 786436
  420.7 1.4 copy-start
  420.7 71.9 %copy-start.2 = (f32[512,512]{1,0:T(8,128)S(1)}, f32[512,512]{1,0:T(8,128)}, u32[]{:S(2)}) copy-start(f32[512,512]{1,0:T(8,128)} %param.10) | copy-start | bytes 3145732
  422.1 68.7 %reduce-scatter.10.cloned.1.call-start = ((), (), s32[]{:S(2)}) async-start(), calls=%async_computation.8 | async-start | bytes 1179648
  454.2 38.4 %copy-start.4 = (f32[128,512]{1,0:T(8,128)S(1)}, f32[128,512]{1,0:T(8,128)}, u32[]{:S(2)}) copy-start(f32[128,512]{1,0:T(8,128)} %reduce-scatter.6.cloned.1.call-done) | copy-start | bytes 786436
  456.9 255.7 %reduce-scatter.8.cloned.1.call-start = ((), (), s32[]{:S(2)}) async-start(), calls=%async_computation.7 | async-start | bytes 270336 | tf_op jit(solution)/shard_map/reduce_scatter | solution.py:116
Sparse Core Ops, SparseCore 0:
  10.4 27.1 all-gather.2
  40.2 83.2 all-gather.4
  128.4 213.2 all-reduce.1
  422.2 31.9 reduce-scatter.5
  457.1 33.7 reduce-scatter.9
  494.5 218.0 reduce-scatter.7
where the time goes:
time: 722 us; the launch traced here: 721 us
  waiting for transfers between devices  518 us (72%)
  other arithmetic  105 us (15%)
  matrix products  47 us (7%)
  local copies, waits for them, and re-layouts  36 us (5%)
  between operations  14.2 us (2%)
    reduce_scatter x1, waiting for transfers between devices, on_device(): lax.psum_scatter(weight_part, 'col', scatter_dimension=1, tiled=True)  219 us
    psum x1, waiting for transfers between devices, on_device(): full_sums = lax.psum(partial_value, 'col')  213 us
    scatter-add x3, other arithmetic, add_group(): return (totals.at[row_ids].add(products), None)  56.7 us
    scatter-add x3, other arithmetic, add_group(): return (totals.at[col_ids].add(products), None)  34.9 us
    unnamed x7, waiting for transfers between devices  32.9 us
    reduce_scatter x1, waiting for transfers between devices, on_device(): lax.psum_scatter(column_part, 'row', scatter_dimension=0, tiled=True)  32 us
    dot_general x3, matrix products, add_group(): jnp.einsum('sab,sbc->sac', group_vals, selected, preferred_element_type=j...  21.3 us
    dot_general x3, matrix products, add_group(): jnp.einsum('sab,sac->sbc', group_vals, selected, preferred_element_type=j...  21.2 us
  transfers between devices with their start and end apart: 6, of which 5 were waited for; matrix products, arithmetic and copies ran while one was open for 14% of the time, Pallas kernels for 0%

commit v1 on v0

--- a/solution.py
+++ b/solution.py
@@ -95,7 +95,11 @@
         column_rows.reshape(col_blocks, block, hidden_width),
         row_blocks,
     )
-    full_sums = lax.psum(partial_value, "col")
+    full_sums = partial_value
+    for hop in (1, 2, 4, 8, 16):
+        full_sums = full_sums + lax.ppermute(
+            full_sums, "col", [(dev, dev ^ hop) for dev in range(32)]
+        )
     row_start = lax.axis_index("col") * own_rows
     own_sums = lax.dynamic_slice_in_dim(full_sums, row_start, own_rows, 0)
     activated = jax.nn.silu(own_sums)

time: 722 us -> 1880 us (2.60)
  waiting for transfers between devices: 518 us -> 1610 us
  other arithmetic: 105 us -> 153 us
    ppermute x0 -> x5, waiting for transfers between devices: none -> 903 us  [on_device(): lax.ppermute(full_sums, 'col', [(dev, dev ^ hop) for dev in range(32)])]
    all_gather x1, waiting for transfers between devices: 0.02 us -> 409 us  [on_device(): gathered_cot = lax.all_gather(cotangent, 'col', axis=0, tiled=True)]
    psum x1 -> x0, waiting for transfers between devices: 213 us -> none  [on_device(): full_sums = lax.psum(partial_value, 'col')]
    add x0 -> x4, other arithmetic: none -> 44.4 us  [on_device(): full_sums + lax.ppermute(full_sums, 'col', [(dev, dev ^ hop) for dev in r...]
  transfers between devices with their start and end apart: 6 -> 10, of which waited for: 5 -> 9; matrix products, arithmetic and copies ran while one was open for 14% -> 1% of each run, Pallas kernels for 0% -> 0%
where the time goes in v1:
time: 1880 us
  waiting for transfers between devices  1610 us (86%)
  other arithmetic  153 us (8%)
  matrix products  47.8 us (3%)
  local copies, waits for them, and re-layouts  36 us (2%)
    ppermute x5, waiting for transfers between devices, on_device(): lax.ppermute(full_sums, 'col', [(dev, dev ^ hop) for dev in range(32)])  903 us
    all_gather x1, waiting for transfers between devices, on_device(): gathered_cot = lax.all_gather(cotangent, 'col', axis=0, tiled=True)  409 us
    reduce_scatter x1, waiting for transfers between devices, on_device(): lax.psum_scatter(weight_part, 'col', scatter_dimension=1, tiled=True)  216 us
    scatter-add x3, other arithmetic, add_group(): return (totals.at[row_ids].add(products), None)  54.8 us
    add x4, other arithmetic, on_device(): full_sums + lax.ppermute(full_sums, 'col', [(dev, dev ^ hop) for dev in r...  44.4 us
  transfers between devices with their start and end apart: 10, of which 9 were waited for; matrix products, arithmetic and copies ran while one was open for 1% of the time, Pallas kernels for 0%

profile of v1, /device:TPU:2, one launch (start us, length us, event | category | flops | bytes accessed | tf_op | source)
XLA Modules:
  0.0 1876.6 jit_solution(15793965232410773126)
XLA Ops:
  17.6 20.8 %all-gather.3.cloned.1.call-done = bf16[1024,512]{1,0:T(8,128)(2,1)} async-done(((bf16[128,512]{1,0:T(8,128)(2,1)}), bf16[1024,512]{1,0:T(8,128)(2,1)}) %all-gather.3.cloned.1.call-update) | async-done | bytes 1048592 | tf_op jit(solution)/shard_map/all_gather | solution.py:90
  42.7 84.4 %while.20 = (s32[]{:T(128)}, f32[32,128,512]{2,1,0:T(8,128)}, s32[3,32]{1,0:T(4,128)S(1)}, bf16[3,32,128,128]{2,3,1,0:T(8,128)(2,1)}, s32[3,32]{1,0:T(4,128)S(1)}, /*index=5*/bf16[8,128,512]{2,1,0:T(8,128)(2,1)S(1)}, s32[]{:T(128)}) while((s32[]{:T(128)}, f32[32,128,512]{2,1,0:T(8,128)}, s32[3,32]{1,0:T(4,128)S(1)}, ...), condition=%wide.region_2.3_spmd, body=%wide.region_0.2_spmd.sunk | while | flops 541066624 | bytes 47191700 | solution.py:32
  52.6 18.6 scatter_fusion
  74.0 7.1 fusion.40
  81.0 18.3 scatter_fusion
  102.2 7.1 fusion.40
  109.3 17.9 scatter_fusion
  129.9 181.0 %collective-permute-done = f32[4096,512]{1,0:T(8,128)} collective-permute-done((f32[4096,512]{1,0:T(8,128)}, f32[4096,512]{1,0:T(8,128)}, u32[]{:S(2)}, u32[]{:S(2)}) %collective-permute-start) | collective-permute-done | bytes 8388640 | tf_op jit(solution)/shard_map/ppermute | solution.py:100
  310.9 11.1 bitcast_add_fusion
  324.3 181.4 %collective-permute-done.1 = f32[4096,512]{1,0:T(8,128)} collective-permute-done((f32[4096,512]{1,0:T(8,128)}, f32[4096,512]{1,0:T(8,128)}, u32[]{:S(2)}, u32[]{:S(2)}) %collective-permute-start.1) | collective-permute-done | bytes 8388640 | tf_op jit(solution)/shard_map/ppermute | solution.py:100
  505.7 11.1 add.107
  517.3 180.8 %collective-permute-done.2 = f32[4096,512]{1,0:T(8,128)} collective-permute-done((f32[4096,512]{1,0:T(8,128)}, f32[4096,512]{1,0:T(8,128)}, u32[]{:S(2)}, u32[]{:S(2)}) %collective-permute-start.2) | collective-permute-done | bytes 8388640 | tf_op jit(solution)/shard_map/ppermute | solution.py:100
  698.1 11.1 add.108
  712.9 359.4 %collective-permute-done.3 = f32[4096,512]{1,0:T(8,128)} collective-permute-done((f32[4096,512]{1,0:T(8,128)}, f32[4096,512]{1,0:T(8,128)}, u32[]{:S(2)}, u32[]{:S(2)}) %collective-permute-start.3) | collective-permute-done | bytes 8388640 | tf_op jit(solution)/shard_map/ppermute | solution.py:100
  1072.3 11.1 add.109
  1087.6 409.1 %all-gather.5.cloned.1.call-done = bf16[4096,512]{1,0:T(8,128)(2,1)} async-done(((bf16[128,512]{1,0:T(8,128)(2,1)}), bf16[4096,512]{1,0:T(8,128)(2,1)}) %all-gather.5.cloned.1.call-update) | async-done | bytes 4194320 | tf_op jit(solution)/shard_map/all_gather | solution.py:86
  1496.7 12.0 multiply_convert_fusion
  1509.0 71.2 %while.21 = (s32[]{:T(128)}, f32[8,128,512]{2,1,0:T(8,128)S(1)}, s32[3,32]{1,0:T(4,128)S(1)}, bf16[3,32,128,128]{2,3,1,0:T(8,128)(2,1)}, s32[3,32]{1,0:T(4,128)S(1)}, /*index=5*/bf16[32,128,512]{2,1,0:T(8,128)(2,1)}, s32[]{:T(128)}) while((s32[]{:T(128)}, f32[8,128,512]{2,1,0:T(8,128)S(1)}, s32[3,32]{1,0:T(4,128)S(1)}, ...), condition=%wide.region_5.6_spmd, body=%wide.region_3.5_spmd.sunk | while | flops 541066624 | bytes 47191700 | solution.py:60
  1521.1 11.8 scatter_fusion.1
  1545.0 11.6 scatter_fusion.1
  1568.7 11.5 scatter_fusion.1
  1581.7 30.0 %reduce-scatter.6.cloned.1.call-done = f32[128,512]{1,0:T(8,128)} async-done(((f32[1024,512]{1,0:T(8,128)}), f32[128,512]{1,0:T(8,128)}) %reduce-scatter.6.cloned.1.call-update) | async-done | bytes 262160 | tf_op jit(solution)/shard_map/reduce_scatter | solution.py:114
  1616.1 32.2 %reduce-scatter.10.cloned.1.call-done = f32[64,512]{1,0:T(8,128)} async-done(((f32[512,512]{1,0:T(8,128)}), f32[64,512]{1,0:T(8,128)}) %reduce-scatter.10.cloned.1.call-update) | async-done | bytes 131088
  1652.0 216.1 %reduce-scatter.8.cloned.1.call-done = f32[64,16]{0,1:T(8,128)} async-done(((f32[64,512]{0,1:T(8,128)}), f32[64,16]{0,1:T(8,128)}) %reduce-scatter.8.cloned.1.call-update) | async-done | bytes 4112 | tf_op jit(solution)/shard_map/reduce_scatter | solution.py:120
  (68 shorter events, 90.0 us)
Async XLA Ops:
  8.0 30.4 %all-gather.3.cloned.1.call-start = ((), (), s32[]{:S(2)}) async-start(), calls=%async_computation.3 | async-start | bytes 1179648 | tf_op jit(solution)/shard_map/all_gather | solution.py:90
  10.3 1486.4 %all-gather.5.cloned.1.call-start = ((), (), s32[]{:S(2)}) async-start(), calls=%async_computation.4 | async-start | bytes 4325376 | tf_op jit(solution)/shard_map/all_gather | solution.py:86
  38.4 4.3 copy-start.1
  127.1 183.8 %collective-permute-start = (f32[4096,512]{1,0:T(8,128)}, f32[4096,512]{1,0:T(8,128)}, u32[]{:S(2)}, u32[]{:S(2)}) collective-permute-start(f32[4096,512]{1,0:T(8,128)} %bitcast.62), channel_id=1, source_target_pairs={{0,1},{1,0},{2,3},{3,2},{4,5},{5,4},{6,7},{7,6},{8,9},{9,8},{10,11... | collective-permute-start | bytes 25165832 | tf_op jit(solution)/shard_map/ppermute | solution.py:100
  322.0 183.7 %collective-permute-start.1 = (f32[4096,512]{1,0:T(8,128)}, f32[4096,512]{1,0:T(8,128)}, u32[]{:S(2)}, u32[]{:S(2)}) collective-permute-start(f32[4096,512]{1,0:T(8,128)} %bitcast_add_fusion), channel_id=1, source_target_pairs={{0,2},{1,3},{2,0},{3,1},{4,6},{5,7},{6,4},{7,5},{8,10},{9,11},{10,... | collective-permute-start | bytes 25165832 | tf_op jit(solution)/shard_map/ppermute | solution.py:100
  516.8 181.4 %collective-permute-start.2 = (f32[4096,512]{1,0:T(8,128)}, f32[4096,512]{1,0:T(8,128)}, u32[]{:S(2)}, u32[]{:S(2)}) collective-permute-start(f32[4096,512]{1,0:T(8,128)} %add.107), channel_id=1, source_target_pairs={{0,4},{1,5},{2,6},{3,7},{4,0},{5,1},{6,2},{7,3},{8,12},{9,13},{10,... | collective-permute-start | bytes 25165832 | tf_op jit(solution)/shard_map/ppermute | solution.py:100
  709.2 363.0 %collective-permute-start.3 = (f32[4096,512]{1,0:T(8,128)}, f32[4096,512]{1,0:T(8,128)}, u32[]{:S(2)}, u32[]{:S(2)}) collective-permute-start(f32[4096,512]{1,0:T(8,128)} %add.108), channel_id=1, source_target_pairs={{0,8},{1,9},{2,10},{3,11},{4,12},{5,13},{6,14},{7,15},{8,0},{9,1},... | collective-permute-start | bytes 25165832 | tf_op jit(solution)/shard_map/ppermute | solution.py:100
  1083.4 413.3 %collective-permute-start.4 = (f32[4096,512]{1,0:T(8,128)}, f32[4096,512]{1,0:T(8,128)}, u32[]{:S(2)}, u32[]{:S(2)}) collective-permute-start(f32[4096,512]{1,0:T(8,128)} %add.109), channel_id=1, source_target_pairs={{0,16},{1,17},{2,18},{3,19},{4,20},{5,21},{6,22},{7,23},{8,24},{9,... | collective-permute-start | bytes 25165832 | tf_op jit(solution)/shard_map/ppermute | solution.py:100
  1087.5 524.2 %reduce-scatter.6.cloned.1.call-start = ((), (), s32[]{:S(2)}) async-start(), calls=%async_computation.5 | async-start | bytes 2359296 | tf_op jit(solution)/shard_map/reduce_scatter | solution.py:114
  1509.0 102.7 %copy-start.3 = (f32[128,512]{1,0:T(8,128)S(1)}, f32[128,512]{1,0:T(8,128)}, u32[]{:S(2)}) copy-start(f32[128,512]{1,0:T(8,128)} %param.9) | copy-start | bytes 786436
  1580.2 1.4 copy-start
  1580.3 69.8 %copy-start.2 = (f32[512,512]{1,0:T(8,128)S(1)}, f32[512,512]{1,0:T(8,128)}, u32[]{:S(2)}) copy-start(f32[512,512]{1,0:T(8,128)} %param.10) | copy-start | bytes 3145732
  1581.6 66.7 %reduce-scatter.10.cloned.1.call-start = ((), (), s32[]{:S(2)}) async-start(), calls=%async_computation.7 | async-start | bytes 1179648
  1614.3 253.9 %reduce-scatter.8.cloned.1.call-start = ((), (), s32[]{:S(2)}) async-start(), calls=%async_computation.6 | async-start | bytes 270336 | tf_op jit(solution)/shard_map/reduce_scatter | solution.py:120
Sparse Core Ops, SparseCore 0:
  11.2 27.1 all-gather.2
  1581.7 29.9 reduce-scatter.5
  1614.4 33.8 reduce-scatter.9
Sparse Core Ops, SparseCore 1:
  1087.6 409.0 all-gather.4
  1650.1 218.0 reduce-scatter.7
